TPU v7x, 32 devices: a whole 2x2x4 slice. The times are simulated.
32 devices in a mesh: kset: 2 (over y), grid: 16 (over z, x, core).
Axes of the slice: x: 2, y: 2, z: 4, core: 2. Of those that a mesh axis runs over, the one named last changes fastest.
Arguments:
- bands: bfloat16 [4, 4096, 1536], P('kset', 'grid'), parts along dimension 0, may hold values from -4 to 4, as said below
- hbands: bfloat16 [4, 4096, 1536], P('kset', 'grid'), parts along dimension 0, may hold values from -10 to 10, as said below
- occupied: int32 [4], P('kset'), parts along dimension 0, may hold values from 192 to 576
Outputs:
- new_bands: bfloat16 [4, 4096, 1536], P('kset', 'grid'), parts along dimension 0
There are 2 independent parts, one for each index of `kset`. A program takes and returns all parts, laid end to end along the dimension named above; each array names one. Nothing has to cross between parts.
Inputs may be any that keep to these rules, and one draw needn't show every extreme that they name: `bands`: real values on every grid point. `hbands`: real values on every grid point.
All inputs are finite; a program needn't handle non-finite values.
Results may differ from a plain program's by a relative error of at most 0.0079.
Values may be sent and summed in bfloat16 or wider, within the bound.
A program may use at most 64 MiB of HBM per device.

v0:
```python
import jax
import jax.numpy as jnp
from jax import lax
from jax.sharding import PartitionSpec as P

MCW = 2


def embedding(full):
    width = full.shape[-1] // 2
    real_part = full[..., :width]
    imag_part = full[..., width:]
    upper = jnp.concatenate([real_part, imag_part], -1)
    lower = jnp.concatenate([-imag_part, real_part], -1)
    return jnp.concatenate([upper, lower], -2)


def on_device(bands, hbands, occupied):
    points, local_rows, columns = bands.shape
    half = columns // 2
    devices = lax.axis_size("grid")
    share = half // devices
    scale = 1.0 / (2.0 * local_rows * devices)
    blocks = []
    for point in range(points):
        start = jnp.int32(0)
        count = lax.axis_size("grid") * share
        band_k = bands[point]
        hband_k = hbands[point]
        band_cols = jnp.concatenate(
            [
                lax.dynamic_slice_in_dim(band_k, start, count, 1),
                lax.dynamic_slice_in_dim(band_k, half, count, 1),
            ],
            1,
        )
        summed = jnp.einsum("gi,gj->ij", band_cols, hband_k, preferred_element_type=jnp.float32)
        hband_cols = jnp.concatenate(
            [
                lax.dynamic_slice_in_dim(hband_k, start, count, 1),
                lax.dynamic_slice_in_dim(hband_k, half, count, 1),
            ],
            1,
        )
        summed = summed + jnp.einsum(
            "gi,gj->ij", hband_cols, band_k, preferred_element_type=jnp.float32
        )
        real_rows = (summed[:count, :half] + summed[count:, half:]) * scale
        imag_rows = (summed[:count, half:] - summed[count:, :half]) * scale
        blocks.append(
            lax.psum_scatter(
                jnp.concatenate([real_rows, imag_rows], 1), "grid", scatter_dimension=0, tiled=True
            )
        )
    hamiltonian = jnp.stack(blocks, 1)
    hamiltonian = jnp.transpose(hamiltonian, (1, 0, 2))
    ham_real = hamiltonian[:, :, :half]
    ham_imag = hamiltonian[:, :, half:]
    row_index = lax.axis_index("grid") * share + lax.iota(jnp.int32, share)
    col_index = lax.iota(jnp.int32, half)
    identity = (row_index[:, None] == col_index[None, :]).astype(jnp.float32)[None]
    trace_part = jnp.sum(ham_real * identity, axis=(1, 2))
    trace = lax.psum(trace_part, "grid")
    level = (trace / half)[:, None, None]
    centred = ham_real - level * identity
    squares = jnp.sum(centred * centred, axis=(1, 2)) + jnp.sum(ham_imag * ham_imag, axis=(1, 2))
    total = lax.psum(squares, "grid")
    spread = jnp.sqrt(total / half + 1e-06)[:, None, None]
    filling = (occupied.astype(jnp.float32) / half)[:, None, None]
    dens_real = filling * identity - centred / (4.0 * spread)
    dens_imag = -ham_imag / (4.0 * spread)
    density = jnp.concatenate([dens_real, dens_imag], 2).astype(jnp.bfloat16)
    for repeat in range(MCW):
        gathered = lax.all_gather(density, "grid", axis=1, tiled=True)
        matrix = embedding(gathered)
        square = jnp.einsum("krc,kcd->krd", density, matrix, preferred_element_type=jnp.float32)
        cube = jnp.einsum(
            "krc,kcd->krd", square.astype(jnp.bfloat16), matrix, preferred_element_type=jnp.float32
        )
        density = (3.0 * square - 2.0 * cube).astype(jnp.bfloat16)
    gathered = lax.all_gather(density, "grid", axis=1, tiled=True)
    matrix = embedding(gathered)
    updated = jnp.einsum("kgc,kcd->kgd", bands, matrix, preferred_element_type=jnp.float32)
    return updated.astype(jnp.bfloat16)


def solution(mesh):
    return jax.shard_map(
        on_device,
        mesh=mesh,
        in_specs=(P("kset", "grid", None), P("kset", "grid", None), P("kset")),
        out_specs=P("kset", "grid", None),
        check_vma=False,
    )
```

profile of v0, /device:TPU:0, one launch (start us, length us, event | category | flops | bytes accessed | tf_op | source)
XLA Modules:
  0.0 426.6 jit_solution(12887339969295550722)
XLA Ops:
  6.5 0.0 copy-start.1
  6.5 0.0 copy-start
  6.5 0.0 reduce-scatter.7.cloned.1.call-start
  6.5 3.0 fusion.32
  9.5 0.0 copy-done.1
  9.5 0.0 copy-done
  9.5 1.5 convolution_add_fusion.1
  11.0 0.6 fusion.23
  11.6 2.5 pad_maximum_fusion
  14.1 6.1 %copy.18 = f32[768,1536]{1,0:T(8,128)} copy(f32[768,1536]{0,1:T(8,128)} %pad_maximum_fusion) | data formatting | bytes 9437184
  20.1 0.0 reduce-scatter.7.cloned.1.call-update
  20.1 0.0 reduce-scatter.9.cloned.1.call-start
  20.2 1.4 fusion.27
  21.6 1.5 convolution_add_fusion
  23.1 0.6 fusion.21
  23.7 2.5 pad_maximum_fusion.1
  26.2 6.2 %copy.20 = f32[768,1536]{1,0:T(8,128)} copy(f32[768,1536]{0,1:T(8,128)} %pad_maximum_fusion.1) | data formatting | bytes 9437184
  32.4 0.0 copy-start.5
  32.4 0.0 reduce-scatter.9.cloned.1.call-update
  32.5 0.0 all-gather.4.cloned.1.call-start
  32.5 0.1 fusion.46
  32.6 65.9 %reduce-scatter.7.cloned.1.call-done = f32[48,1536]{1,0:T(8,128)} async-done(((f32[768,1536]{1,0:T(8,128)}), f32[48,1536]{1,0:T(8,128)}) %reduce-scatter.7.cloned.1.call-update) | async-done | bytes 294928
  98.5 1.2 copy.19
  99.7 0.2 copy.9
  100.0 77.6 %reduce-scatter.9.cloned.1.call-done = f32[48,1536]{1,0:T(8,128)} async-done(((f32[768,1536]{1,0:T(8,128)}), f32[48,1536]{1,0:T(8,128)}) %reduce-scatter.9.cloned.1.call-update) | async-done | bytes 294928
  177.6 1.2 copy.21
  178.8 0.2 copy.10
  179.1 0.1 multiply_reduce_fusion.2
  179.2 30.0 %psum.14 = f32[2]{0:T(128)S(1)} all-reduce(f32[2]{0:T(128)S(1)} %multiply_reduce_fusion.2), channel_id=1, replica_groups=mesh['kset'=2,'grid'=16] {'grid'}, use_global_device_ids=true, to_apply=%region_3.0 | all-reduce | flops 2 | bytes 16 | tf_op jit(solution)/shard_map/psum | solution.py:63
  209.2 0.2 multiply_reduce_fusion
  209.4 0.0 copy-done.5
  209.4 29.5 %psum.15 = f32[2]{0:T(128)S(1)} all-reduce(f32[2]{0:T(128)S(1)} %add.42), channel_id=1, replica_groups=mesh['kset'=2,'grid'=16] {'grid'}, use_global_device_ids=true, to_apply=%region_6.0 | all-reduce | flops 2 | bytes 16 | tf_op jit(solution)/shard_map/psum | solution.py:67
  238.9 0.2 subtract_convert_fusion
  239.1 1.0 copy.11
  240.1 0.0 all-gather.4.cloned.1.call-update
  240.2 0.2 all-gather.6.cloned.1.call-start
  240.4 50.4 %all-gather.4.cloned.1.call-done = bf16[2,768,1536]{2,0,1:T(2,128)(2,1)} async-done(((bf16[2,48,1536]{2,0,1:T(2,128)(2,1)}), bf16[2,768,1536]{2,0,1:T(2,128)(2,1)}) %all-gather.4.cloned.1.call-update) | async-done | bytes 4718608 | tf_op jit(solution)/shard_map/all_gather | solution.py:74
  290.8 3.1 copy.14
  293.9 0.3 slice_negate_fusion.2
  294.2 1.9 fusion.9
  296.0 2.5 fusion.25
  298.6 0.0 all-gather.6.cloned.1.call-update
  298.6 0.0 copy-start.4
  298.6 0.0 all-gather.8.cloned.1.call-start
  298.6 51.9 %all-gather.6.cloned.1.call-done = bf16[2,768,1536]{2,1,0:T(8,128)(2,1)} async-done(((bf16[2,48,1536]{2,1,0:T(8,128)(2,1)}), bf16[2,768,1536]{2,1,0:T(8,128)(2,1)}) %all-gather.6.cloned.1.call-update) | async-done | bytes 4718608 | tf_op jit(solution)/shard_map/all_gather | solution.py:74
  350.6 0.0 copy-start.2
  350.6 2.8 slice_negate_fusion.1
  353.4 0.0 copy-done.4
  353.4 0.9 copy-done.2
  354.3 1.9 fusion.7
  356.2 2.5 fusion.24
  358.7 0.0 all-gather.8.cloned.1.call-update
  358.7 52.0 %all-gather.8.cloned.1.call-done = bf16[2,768,1536]{2,1,0:T(8,128)(2,1)} async-done(((bf16[2,48,1536]{2,1,0:T(8,128)(2,1)}), bf16[2,768,1536]{2,1,0:T(8,128)(2,1)}) %all-gather.8.cloned.1.call-update) | async-done | bytes 4718608 | tf_op jit(solution)/shard_map/all_gather | solution.py:81
  410.7 0.0 copy-start.3
  410.7 2.8 slice_negate_fusion
  413.5 0.9 copy-done.3
  414.4 4.0 fusion.13
  418.4 1.6 copy.16
  (7 shorter events, 0.1 us)
Async XLA Ops:
  6.5 3.0 copy-start.1
  6.5 3.0 copy-start
  6.5 92.0 %reduce-scatter.7.cloned.1.call-start = ((), (), s32[]{:S(2)}) async-start(), calls=%async_computation.5 | async-start | bytes 5013504
  20.1 157.4 %reduce-scatter.9.cloned.1.call-start = ((), (), s32[]{:S(2)}) async-start(), calls=%async_computation.6 | async-start | bytes 5013504
  32.4 177.0 %copy-start.5 = (s32[2]{0:T(128)S(1)}, s32[2]{0:T(128)}, u32[]{:S(2)}) copy-start(s32[2]{0:T(128)} %param.5) | copy-start | bytes 28
  32.5 258.3 %all-gather.4.cloned.1.call-start = ((), (), s32[]{:S(2)}) async-start(), calls=%async_computation.2 | async-start | bytes 5013504 | tf_op jit(solution)/shard_map/all_gather | solution.py:74
  240.2 110.4 %all-gather.6.cloned.1.call-start = ((), (), s32[]{:S(2)}) async-start(), calls=%async_computation.3 | async-start | bytes 5013504 | tf_op jit(solution)/shard_map/all_gather | solution.py:74
  298.6 54.8 %copy-start.4 = (bf16[2,48,1536]{2,1,0:T(8,128)(2,1)S(1)}, bf16[2,48,1536]{2,1,0:T(8,128)(2,1)}, u32[]{:S(2)}) copy-start(bf16[2,48,1536]{2,1,0:T(8,128)(2,1)} %fusion.25) | copy-start | bytes 884740
  298.6 112.1 %all-gather.8.cloned.1.call-start = ((), (), s32[]{:S(2)}) async-start(), calls=%async_computation.4 | async-start | bytes 5013504 | tf_op jit(solution)/shard_map/all_gather | solution.py:81
  350.6 3.8 copy-start.2
  410.7 3.8 copy-start.3
Sparse Core Ops, SparseCore 0:
  20.3 78.2 reduce-scatter.6
  102.9 74.6 reduce-scatter.8
  240.3 50.4 all-gather.3
  298.7 51.8 all-gather.5
  358.9 51.7 all-gather.7
where the time goes:
time: 427 us
  waiting for transfers between devices  298 us (70%)
  blocking collectives  59.5 us (14%)
  local copies, waits for them, and re-layouts  22.7 us (5%)
  matrix products  20.1 us (5%)
  between operations  13.3 us (3%)
  other arithmetic  12.8 us (3%)
    all_gather x3, waiting for transfers between devices, on_device(): gathered = lax.all_gather(density, 'grid', axis=1, tiled=True)  154 us
    unnamed x7, waiting for transfers between devices  144 us
    psum x1, blocking collectives, on_device(): trace = lax.psum(trace_part, 'grid')  30 us
    psum x1, blocking collectives, on_device(): total = lax.psum(squares, 'grid')  29.5 us
    unnamed x16, local copies, waits for them, and re-layouts  16.5 us
  transfers between devices with their start and end apart: 5, of which 5 were waited for; matrix products, arithmetic and copies ran while one was open for 3% of the time, Pallas kernels for 0%

commit v1 on v0

--- a/solution.py
+++ b/solution.py
@@ -71,7 +71,16 @@
     dens_imag = -ham_imag / (4.0 * spread)
     density = jnp.concatenate([dens_real, dens_imag], 2).astype(jnp.bfloat16)
     for repeat in range(MCW):
-        gathered = lax.all_gather(density, "grid", axis=1, tiled=True)
+        ways = lax.axis_size("grid")
+        up = [(d, (d + 1) % ways) for d in range(ways)]
+        down = [(d, (d - 1) % ways) for d in range(ways)]
+        earlier, later = ([density], [density])
+        for _ in range(ways // 2):
+            earlier.append(lax.ppermute(earlier[-1], "grid", up))
+        for _ in range((ways - 1) // 2):
+            later.append(lax.ppermute(later[-1], "grid", down))
+        line = jnp.concatenate([*earlier[::-1], *later[1:]], axis=1)
+        gathered = jnp.roll(line, (lax.axis_index("grid") - ways // 2) * density.shape[1], axis=1)
         matrix = embedding(gathered)
         square = jnp.einsum("krc,kcd->krd", density, matrix, preferred_element_type=jnp.float32)
         cube = jnp.einsum(

time: 427 us -> 480 us (1.12)
  starting transfers between devices: 0.35 us -> 63.5 us
  waiting for transfers between devices: 298 us -> 276 us
  other arithmetic: 12.8 us -> 20.4 us
    all_gather x3 -> x1, waiting for transfers between devices: 154 us -> 54.1 us  [on_device(): gathered = lax.all_gather(density, 'grid', axis=1, tiled=True)]
    ppermute x0 -> x30, waiting for transfers between devices: none -> 78.4 us  [the longest x16 75 us: on_device(): earlier.append(lax.ppermute(earlier[-1], 'grid', up))]
    ppermute x0 -> x30, starting transfers between devices: none -> 63.4 us  [the longest x14 63.2 us: on_device(): later.append(lax.ppermute(later[-1], 'grid', down))]
    concatenate x0 -> x2, other arithmetic: none -> 10 us  [on_device(): jnp.roll(line, (lax.axis_index('grid') - ways // 2) * density.shape[1], a...]
    unnamed x16 -> x55, local copies, waits for them, and re-layouts: 16.5 us -> 24.4 us
    unnamed x7 -> x5, waiting for transfers between devices: 144 us -> 144 us
  transfers between devices with their start and end apart: 5 -> 33, of which waited for: 5 -> 22; matrix products, arithmetic and copies ran while one was open for 3% -> 4% of each run, Pallas kernels for 0% -> 0%
where the time goes in v1:
time: 480 us; the launch traced here: 479 us
  waiting for transfers between devices  276 us (58%)
  starting transfers between devices  63.5 us (13%)
  blocking collectives  59.5 us (12%)
  local copies, waits for them, and re-layouts  26.5 us (6%)
  other arithmetic  20.4 us (4%)
  matrix products  19.5 us (4%)
  between operations  13.6 us (3%)
    unnamed x5, waiting for transfers between devices  144 us
    ppermute x16, waiting for transfers between devices, on_device(): earlier.append(lax.ppermute(earlier[-1], 'grid', up))  75 us
    ppermute x14, starting transfers between devices, on_device(): later.append(lax.ppermute(later[-1], 'grid', down))  63.2 us
    all_gather x1, waiting for transfers between devices, on_device(): gathered = lax.all_gather(density, 'grid', axis=1, tiled=True)  54.1 us
    psum x1, blocking collectives, on_device(): trace = lax.psum(trace_part, 'grid')  30 us
    psum x1, blocking collectives, on_device(): total = lax.psum(squares, 'grid')  29.5 us
    unnamed x55, local copies, waits for them, and re-layouts  24.4 us
    concatenate x2, other arithmetic, on_device(): jnp.roll(line, (lax.axis_index('grid') - ways // 2) * density.shape[1], a...  10 us
  transfers between devices with their start and end apart: 33, of which 22 were waited for; matrix products, arithmetic and copies ran while one was open for 4% of the time, Pallas kernels for 0%

profile of v1, /device:TPU:0, one launch (start us, length us, event | category | flops | bytes accessed | tf_op | source)
XLA Modules:
  0.0 479.0 jit_solution(8477917129008728734)
XLA Ops:
  6.5 3.0 fusion.30
  9.5 1.5 convolution_add_fusion.1
  11.6 2.5 pad_maximum_fusion
  14.1 6.1 %copy.14 = f32[768,1536]{1,0:T(8,128)} copy(f32[768,1536]{0,1:T(8,128)} %pad_maximum_fusion) | data formatting | bytes 9437184
  20.2 1.4 fusion.25
  21.7 1.5 convolution_add_fusion
  23.7 2.5 pad_maximum_fusion.1
  26.3 6.2 %copy.16 = f32[768,1536]{1,0:T(8,128)} copy(f32[768,1536]{0,1:T(8,128)} %pad_maximum_fusion.1) | data formatting | bytes 9437184
  32.6 65.9 %reduce-scatter.7.cloned.1.call-done = f32[48,1536]{1,0:T(8,128)} async-done(((f32[768,1536]{1,0:T(8,128)}), f32[48,1536]{1,0:T(8,128)}) %reduce-scatter.7.cloned.1.call-update) | async-done | bytes 294928
  98.5 1.2 copy.15
  100.0 77.6 %reduce-scatter.9.cloned.1.call-done = f32[48,1536]{1,0:T(8,128)} async-done(((f32[768,1536]{1,0:T(8,128)}), f32[48,1536]{1,0:T(8,128)}) %reduce-scatter.9.cloned.1.call-update) | async-done | bytes 294928
  177.6 1.2 copy.17
  179.2 30.0 %psum.14 = f32[2]{0:T(128)S(1)} all-reduce(f32[2]{0:T(128)S(1)} %multiply_reduce_fusion.2), channel_id=1, replica_groups=mesh['kset'=2,'grid'=16] {'grid'}, use_global_device_ids=true, to_apply=%region_3.0 | all-reduce | flops 2 | bytes 16 | tf_op jit(solution)/shard_map/psum | solution.py:63
  209.5 29.5 %psum.15 = f32[2]{0:T(128)S(1)} all-reduce(f32[2]{0:T(128)S(1)} %add.51), channel_id=1, replica_groups=mesh['kset'=2,'grid'=16] {'grid'}, use_global_device_ids=true, to_apply=%region_6.0 | all-reduce | flops 2 | bytes 16 | tf_op jit(solution)/shard_map/psum | solution.py:67
  239.2 8.8 %collective-permute-done = bf16[2,48,1536]{2,1,0:T(8,128)(2,1)S(1)} collective-permute-done((bf16[2,48,1536]{2,1,0:T(8,128)(2,1)S(1)}, bf16[2,48,1536]{2,1,0:T(8,128)(2,1)S(1)}, u32[]{:S(2)}, u32[]{:S(2)}) %collective-permute-start) | collective-permute-done | bytes 294944 | tf_op jit(solution)/shard_map/ppermute | solution.py:79
  248.1 4.4 collective-permute-start.8
  252.5 4.4 collective-permute-done.1
  256.9 4.5 collective-permute-start.9
  261.4 4.4 collective-permute-done.2
  265.9 4.5 collective-permute-start.10
  270.4 4.4 collective-permute-done.3
  275.5 4.5 collective-permute-start.11
  280.1 3.7 collective-permute-done.4
  285.0 4.7 collective-permute-start.12
  289.7 3.0 collective-permute-done.5
  292.7 1.3 collective-permute-done.12
  294.0 4.8 %collective-permute-start.13 = (bf16[2,48,1536]{2,1,0:T(8,128)(2,1)}, bf16[2,48,1536]{2,1,0:T(8,128)(2,1)}, u32[]{:S(2)}, u32[]{:S(2)}) collective-permute-start(bf16[2,48,1536]{2,1,0:T(8,128)(2,1)} %collective-permute-done.12), channel_id=1, source_target_pairs={{0,15},{1,0},{2,1},{3,2},{4,3},{5,4},{6,5},{7,6},{8,7},{9,8},{10,9... | collective-permute-start | bytes 884744 | tf_op jit(solution)/shard_map/ppermute | solution.py:81
  298.8 3.0 collective-permute-done.6
  301.8 1.6 collective-permute-done.13
  303.3 4.6 collective-permute-start.14
  307.9 3.0 collective-permute-done.7
  310.9 1.0 constant_dynamic-update-slice_fusion.15
  311.9 1.0 constant_dynamic-update-slice_fusion.14
  312.9 1.0 constant_dynamic-update-slice_fusion.13
  313.9 1.0 constant_dynamic-update-slice_fusion.12
  314.9 1.0 constant_dynamic-update-slice_fusion.11
  316.1 1.0 constant_dynamic-update-slice_fusion.2
  317.1 1.0 constant_dynamic-update-slice_fusion.1
  318.1 5.0 %fusion.7 = bf16[2,768,1536]{2,1,0:T(8,128)(2,1)S(1)} fusion(s32[]{:T(128)S(6)} %select_n.13, bf16[2,768,1536]{2,1,0:T(8,128)(2,1)S(1)} %constant_dynamic-update-slice_fusion), kind=kLoop, calls=%fused_computation.15 | loop fusion | flops 9437184 | bytes 9437188 | tf_op jit(solution)/shard_map/jit(_roll_dynamic)/concatenate | solution.py:83
  323.5 1.9 fusion.11
  325.3 1.9 subtract_convert_fusion.1
  327.3 8.9 %collective-permute-done.15 = bf16[2,48,1536]{2,1,0:T(8,128)(2,1)S(1)} collective-permute-done((bf16[2,48,1536]{2,1,0:T(8,128)(2,1)S(1)}, bf16[2,48,1536]{2,1,0:T(8,128)(2,1)S(1)}, u32[]{:S(2)}, u32[]{:S(2)}) %collective-permute-start.15) | collective-permute-done | bytes 294944 | tf_op jit(solution)/shard_map/ppermute | solution.py:79
  336.2 4.4 collective-permute-start.23
  340.6 4.5 collective-permute-done.16
  345.2 4.4 collective-permute-start.24
  349.6 4.5 collective-permute-done.17
  354.1 4.4 collective-permute-start.25
  358.5 4.5 collective-permute-done.18
  363.1 4.4 collective-permute-start.26
  367.5 4.5 collective-permute-done.19
  372.0 4.4 collective-permute-start.27
  376.4 4.5 collective-permute-done.20
  381.0 4.4 collective-permute-start.28
  385.4 4.5 collective-permute-done.21
  389.9 4.4 collective-permute-start.29
  394.3 4.4 collective-permute-done.22
  399.2 5.0 %fusion.6 = bf16[2,768,1536]{2,1,0:T(8,128)(2,1)S(1)} fusion(s32[]{:T(128)S(6)} %select_n.13, bf16[2,768,1536]{2,1,0:T(8,128)(2,1)S(1)} %constant_dynamic-update-slice_fusion.16), kind=kLoop, calls=%fused_computation.14 | loop fusion | flops 9437184 | bytes 9437188 | tf_op jit(solution)/shard_map/jit(_roll_dynamic)/concatenate | solution.py:83
  404.6 1.9 fusion.9
  406.5 2.5 subtract_convert_fusion
  409.0 54.1 %all-gather.2.cloned.1.call-done = bf16[2,768,1536]{2,1,0:T(8,128)(2,1)} async-done(((bf16[2,48,1536]{2,1,0:T(8,128)(2,1)}), bf16[2,768,1536]{2,1,0:T(8,128)(2,1)}) %all-gather.2.cloned.1.call-update) | async-done | bytes 4718608 | tf_op jit(solution)/shard_map/all_gather | solution.py:90
  463.1 2.8 slice_negate_fusion
  466.0 0.9 copy-done.2
  466.9 4.0 fusion.15
  470.9 1.6 copy.12
  (97 shorter events, 5.9 us)
Async XLA Ops:
  6.5 3.0 copy-start.1
  6.5 3.0 copy-start
  6.5 92.0 %reduce-scatter.7.cloned.1.call-start = ((), (), s32[]{:S(2)}) async-start(), calls=%async_computation.3 | async-start | bytes 5013504
  20.2 157.4 %reduce-scatter.9.cloned.1.call-start = ((), (), s32[]{:S(2)}) async-start(), calls=%async_computation.4 | async-start | bytes 5013504
  32.5 177.0 %copy-start.10 = (s32[2]{0:T(128)S(1)}, s32[2]{0:T(128)}, u32[]{:S(2)}) copy-start(s32[2]{0:T(128)} %param.7) | copy-start | bytes 28
  32.5 430.6 %all-gather.2.cloned.1.call-start = ((), (), s32[]{:S(2)}) async-start(), calls=%async_computation.2 | async-start | bytes 5013504 | tf_op jit(solution)/shard_map/all_gather | solution.py:90
  239.2 8.9 %collective-permute-start = (bf16[2,48,1536]{2,1,0:T(8,128)(2,1)S(1)}, bf16[2,48,1536]{2,1,0:T(8,128)(2,1)S(1)}, u32[]{:S(2)}, u32[]{:S(2)}) collective-permute-start(bf16[2,48,1536]{2,1,0:T(8,128)(2,1)S(1)} %pad_maximum_fusion.2), channel_id=1, source_target_pairs={{0,1},{1,2},{2,3},{3,4},{4,5},{5,6},{6,7},{7,8},{8,9},{9,10},{10,1... | collective-permute-start | bytes 884744 | tf_op jit(solution)/shard_map/ppermute | solution.py:79
  248.0 8.8 %collective-permute-start.1 = (bf16[2,48,1536]{2,1,0:T(8,128)(2,1)S(1)}, bf16[2,48,1536]{2,1,0:T(8,128)(2,1)S(1)}, u32[]{:S(2)}, u32[]{:S(2)}) collective-permute-start(bf16[2,48,1536]{2,1,0:T(8,128)(2,1)S(1)} %collective-permute-done), channel_id=1, source_target_pairs={{0,1},{1,2},{2,3},{3,4},{4,5},{5,6},{6,7},{7,8},{8,9},{9,10},{10,1... | collective-permute-start | bytes 884744 | tf_op jit(solution)/shard_map/ppermute | solution.py:79
  248.1 8.8 %collective-permute-start.8 = (bf16[2,48,1536]{2,1,0:T(8,128)(2,1)S(1)}, bf16[2,48,1536]{2,1,0:T(8,128)(2,1)S(1)}, u32[]{:S(2)}, u32[]{:S(2)}) collective-permute-start(bf16[2,48,1536]{2,1,0:T(8,128)(2,1)S(1)} %pad_maximum_fusion.2), channel_id=1, source_target_pairs={{0,15},{1,0},{2,1},{3,2},{4,3},{5,4},{6,5},{7,6},{8,7},{9,8},{10,9... | collective-permute-start | bytes 884744 | tf_op jit(solution)/shard_map/ppermute | solution.py:81
  256.9 8.9 %collective-permute-start.2 = (bf16[2,48,1536]{2,1,0:T(8,128)(2,1)S(1)}, bf16[2,48,1536]{2,1,0:T(8,128)(2,1)S(1)}, u32[]{:S(2)}, u32[]{:S(2)}) collective-permute-start(bf16[2,48,1536]{2,1,0:T(8,128)(2,1)S(1)} %collective-permute-done.1), channel_id=1, source_target_pairs={{0,1},{1,2},{2,3},{3,4},{4,5},{5,6},{6,7},{7,8},{8,9},{9,10},{10,1... | collective-permute-start | bytes 884744 | tf_op jit(solution)/shard_map/ppermute | solution.py:79
  256.9 8.9 %collective-permute-start.9 = (bf16[2,48,1536]{2,1,0:T(8,128)(2,1)S(1)}, bf16[2,48,1536]{2,1,0:T(8,128)(2,1)S(1)}, u32[]{:S(2)}, u32[]{:S(2)}) collective-permute-start(bf16[2,48,1536]{2,1,0:T(8,128)(2,1)S(1)} %collective-permute-done.8), channel_id=1, source_target_pairs={{0,15},{1,0},{2,1},{3,2},{4,3},{5,4},{6,5},{7,6},{8,7},{9,8},{10,9... | collective-permute-start | bytes 884744 | tf_op jit(solution)/shard_map/ppermute | solution.py:81
  265.8 8.9 %collective-permute-start.3 = (bf16[2,48,1536]{2,1,0:T(8,128)(2,1)S(1)}, bf16[2,48,1536]{2,1,0:T(8,128)(2,1)S(1)}, u32[]{:S(2)}, u32[]{:S(2)}) collective-permute-start(bf16[2,48,1536]{2,1,0:T(8,128)(2,1)S(1)} %collective-permute-done.2), channel_id=1, source_target_pairs={{0,1},{1,2},{2,3},{3,4},{4,5},{5,6},{6,7},{7,8},{8,9},{9,10},{10,1... | collective-permute-start | bytes 884744 | tf_op jit(solution)/shard_map/ppermute | solution.py:79
  265.9 9.0 %collective-permute-start.10 = (bf16[2,48,1536]{2,1,0:T(8,128)(2,1)S(1)}, bf16[2,48,1536]{2,1,0:T(8,128)(2,1)S(1)}, u32[]{:S(2)}, u32[]{:S(2)}) collective-permute-start(bf16[2,48,1536]{2,1,0:T(8,128)(2,1)S(1)} %collective-permute-done.9), channel_id=1, source_target_pairs={{0,15},{1,0},{2,1},{3,2},{4,3},{5,4},{6,5},{7,6},{8,7},{9,8},{10,9... | collective-permute-start | bytes 884744 | tf_op jit(solution)/shard_map/ppermute | solution.py:81
  274.8 19.2 %copy-start.7 = (bf16[2,48,1536]{2,1,0:T(8,128)(2,1)}, bf16[2,48,1536]{2,1,0:T(8,128)(2,1)S(1)}, u32[]{:S(2)}) copy-start(bf16[2,48,1536]{2,1,0:T(8,128)(2,1)S(1)} %collective-permute-done.3) | copy-start | bytes 884740
  274.8 8.9 %collective-permute-start.4 = (bf16[2,48,1536]{2,1,0:T(8,128)(2,1)S(1)}, bf16[2,48,1536]{2,1,0:T(8,128)(2,1)S(1)}, u32[]{:S(2)}, u32[]{:S(2)}) collective-permute-start(bf16[2,48,1536]{2,1,0:T(8,128)(2,1)S(1)} %collective-permute-done.3), channel_id=1, source_target_pairs={{0,1},{1,2},{2,3},{3,4},{4,5},{5,6},{6,7},{7,8},{8,9},{9,10},{10,1... | collective-permute-start | bytes 884744 | tf_op jit(solution)/shard_map/ppermute | solution.py:79
  274.8 0.7 copy-start.3
  275.5 8.8 %collective-permute-start.11 = (bf16[2,48,1536]{2,1,0:T(8,128)(2,1)S(1)}, bf16[2,48,1536]{2,1,0:T(8,128)(2,1)S(1)}, u32[]{:S(2)}, u32[]{:S(2)}) collective-permute-start(bf16[2,48,1536]{2,1,0:T(8,128)(2,1)S(1)} %collective-permute-done.10), channel_id=1, source_target_pairs={{0,15},{1,0},{2,1},{3,2},{4,3},{5,4},{6,5},{7,6},{8,7},{9,8},{10,9... | collective-permute-start | bytes 884744 | tf_op jit(solution)/shard_map/ppermute | solution.py:81
  283.7 15.0 %copy-start.8 = (bf16[2,48,1536]{2,1,0:T(8,128)(2,1)}, bf16[2,48,1536]{2,1,0:T(8,128)(2,1)S(1)}, u32[]{:S(2)}) copy-start(bf16[2,48,1536]{2,1,0:T(8,128)(2,1)S(1)} %collective-permute-done.4) | copy-start | bytes 884740
  283.7 8.9 %collective-permute-start.5 = (bf16[2,48,1536]{2,1,0:T(8,128)(2,1)S(1)}, bf16[2,48,1536]{2,1,0:T(8,128)(2,1)S(1)}, u32[]{:S(2)}, u32[]{:S(2)}) collective-permute-start(bf16[2,48,1536]{2,1,0:T(8,128)(2,1)S(1)} %collective-permute-done.4), channel_id=1, source_target_pairs={{0,1},{1,2},{2,3},{3,4},{4,5},{5,6},{6,7},{7,8},{8,9},{9,10},{10,1... | collective-permute-start | bytes 884744 | tf_op jit(solution)/shard_map/ppermute | solution.py:79
  284.3 0.7 copy-start.5
  285.0 8.9 %collective-permute-start.12 = (bf16[2,48,1536]{2,1,0:T(8,128)(2,1)S(1)}, bf16[2,48,1536]{2,1,0:T(8,128)(2,1)}, u32[]{:S(2)}, u32[]{:S(2)}) collective-permute-start(bf16[2,48,1536]{2,1,0:T(8,128)(2,1)S(1)} %collective-permute-done.11), channel_id=1, source_target_pairs={{0,15},{1,0},{2,1},{3,2},{4,3},{5,4},{6,5},{7,6},{8,7},{9,8},{10,9... | collective-permute-start | bytes 884744 | tf_op jit(solution)/shard_map/ppermute | solution.py:81
  292.7 9.1 %copy-start.9 = (bf16[2,48,1536]{2,1,0:T(8,128)(2,1)}, bf16[2,48,1536]{2,1,0:T(8,128)(2,1)S(1)}, u32[]{:S(2)}) copy-start(bf16[2,48,1536]{2,1,0:T(8,128)(2,1)S(1)} %collective-permute-done.5) | copy-start | bytes 884740
  292.7 9.1 %collective-permute-start.6 = (bf16[2,48,1536]{2,1,0:T(8,128)(2,1)S(1)}, bf16[2,48,1536]{2,1,0:T(8,128)(2,1)}, u32[]{:S(2)}, u32[]{:S(2)}) collective-permute-start(bf16[2,48,1536]{2,1,0:T(8,128)(2,1)S(1)} %collective-permute-done.5), channel_id=1, source_target_pairs={{0,1},{1,2},{2,3},{3,4},{4,5},{5,6},{6,7},{7,8},{8,9},{9,10},{10,1... | collective-permute-start | bytes 884744 | tf_op jit(solution)/shard_map/ppermute | solution.py:79
  294.0 9.4 %collective-permute-start.13 = (bf16[2,48,1536]{2,1,0:T(8,128)(2,1)}, bf16[2,48,1536]{2,1,0:T(8,128)(2,1)}, u32[]{:S(2)}, u32[]{:S(2)}) collective-permute-start(bf16[2,48,1536]{2,1,0:T(8,128)(2,1)} %collective-permute-done.12), channel_id=1, source_target_pairs={{0,15},{1,0},{2,1},{3,2},{4,3},{5,4},{6,5},{7,6},{8,7},{9,8},{10,9... | collective-permute-start | bytes 884744 | tf_op jit(solution)/shard_map/ppermute | solution.py:81
  301.8 9.2 %collective-permute-start.7 = (bf16[2,48,1536]{2,1,0:T(8,128)(2,1)}, bf16[2,48,1536]{2,1,0:T(8,128)(2,1)}, u32[]{:S(2)}, u32[]{:S(2)}) collective-permute-start(bf16[2,48,1536]{2,1,0:T(8,128)(2,1)} %collective-permute-done.6), channel_id=1, source_target_pairs={{0,1},{1,2},{2,3},{3,4},{4,5},{5,6},{6,7},{7,8},{8,9},{9,10},{10,1... | collective-permute-start | bytes 884744 | tf_op jit(solution)/shard_map/ppermute | solution.py:79
  301.8 14.3 %copy-start.4 = (bf16[2,48,1536]{2,1,0:T(8,128)(2,1)S(1)}, bf16[2,48,1536]{2,1,0:T(8,128)(2,1)}, u32[]{:S(2)}) copy-start(bf16[2,48,1536]{2,1,0:T(8,128)(2,1)} %copy-done.3) | copy-start | bytes 884740
  301.8 14.3 %copy-start.6 = (bf16[2,48,1536]{2,1,0:T(8,128)(2,1)S(1)}, bf16[2,48,1536]{2,1,0:T(8,128)(2,1)}, u32[]{:S(2)}) copy-start(bf16[2,48,1536]{2,1,0:T(8,128)(2,1)} %copy-done.5) | copy-start | bytes 884740
  303.3 14.7 %collective-permute-start.14 = (bf16[2,48,1536]{2,1,0:T(8,128)(2,1)}, bf16[2,48,1536]{2,1,0:T(8,128)(2,1)S(1)}, u32[]{:S(2)}, u32[]{:S(2)}) collective-permute-start(bf16[2,48,1536]{2,1,0:T(8,128)(2,1)} %collective-permute-done.13), channel_id=1, source_target_pairs={{0,15},{1,0},{2,1},{3,2},{4,3},{5,4},{6,5},{7,6},{8,7},{9,8},{10,9... | collective-permute-start | bytes 884744 | tf_op jit(solution)/shard_map/ppermute | solution.py:81
  327.2 9.0 %collective-permute-start.15 = (bf16[2,48,1536]{2,1,0:T(8,128)(2,1)S(1)}, bf16[2,48,1536]{2,1,0:T(8,128)(2,1)S(1)}, u32[]{:S(2)}, u32[]{:S(2)}) collective-permute-start(bf16[2,48,1536]{2,1,0:T(8,128)(2,1)S(1)} %subtract_convert_fusion.1), channel_id=1, source_target_pairs={{0,1},{1,2},{2,3},{3,4},{4,5},{5,6},{6,7},{7,8},{8,9},{9,10},{10,1... | collective-permute-start | bytes 884744 | tf_op jit(solution)/shard_map/ppermute | solution.py:79
  336.2 8.9 %collective-permute-start.16 = (bf16[2,48,1536]{2,1,0:T(8,128)(2,1)S(1)}, bf16[2,48,1536]{2,1,0:T(8,128)(2,1)S(1)}, u32[]{:S(2)}, u32[]{:S(2)}) collective-permute-start(bf16[2,48,1536]{2,1,0:T(8,128)(2,1)S(1)} %collective-permute-done.15), channel_id=1, source_target_pairs={{0,1},{1,2},{2,3},{3,4},{4,5},{5,6},{6,7},{7,8},{8,9},{9,10},{10,1... | collective-permute-start | bytes 884744 | tf_op jit(solution)/shard_map/ppermute | solution.py:79
  336.2 9.0 %collective-permute-start.23 = (bf16[2,48,1536]{2,1,0:T(8,128)(2,1)S(1)}, bf16[2,48,1536]{2,1,0:T(8,128)(2,1)S(1)}, u32[]{:S(2)}, u32[]{:S(2)}) collective-permute-start(bf16[2,48,1536]{2,1,0:T(8,128)(2,1)S(1)} %subtract_convert_fusion.1), channel_id=1, source_target_pairs={{0,15},{1,0},{2,1},{3,2},{4,3},{5,4},{6,5},{7,6},{8,7},{9,8},{10,9... | collective-permute-start | bytes 884744 | tf_op jit(solution)/shard_map/ppermute | solution.py:81
  345.1 8.9 %collective-permute-start.17 = (bf16[2,48,1536]{2,1,0:T(8,128)(2,1)S(1)}, bf16[2,48,1536]{2,1,0:T(8,128)(2,1)S(1)}, u32[]{:S(2)}, u32[]{:S(2)}) collective-permute-start(bf16[2,48,1536]{2,1,0:T(8,128)(2,1)S(1)} %collective-permute-done.16), channel_id=1, source_target_pairs={{0,1},{1,2},{2,3},{3,4},{4,5},{5,6},{6,7},{7,8},{8,9},{9,10},{10,1... | collective-permute-start | bytes 884744 | tf_op jit(solution)/shard_map/ppermute | solution.py:79
  345.2 8.9 %collective-permute-start.24 = (bf16[2,48,1536]{2,1,0:T(8,128)(2,1)S(1)}, bf16[2,48,1536]{2,1,0:T(8,128)(2,1)S(1)}, u32[]{:S(2)}, u32[]{:S(2)}) collective-permute-start(bf16[2,48,1536]{2,1,0:T(8,128)(2,1)S(1)} %collective-permute-done.23), channel_id=1, source_target_pairs={{0,15},{1,0},{2,1},{3,2},{4,3},{5,4},{6,5},{7,6},{8,7},{9,8},{10,9... | collective-permute-start | bytes 884744 | tf_op jit(solution)/shard_map/ppermute | solution.py:81
  354.1 8.9 %collective-permute-start.18 = (bf16[2,48,1536]{2,1,0:T(8,128)(2,1)S(1)}, bf16[2,48,1536]{2,1,0:T(8,128)(2,1)S(1)}, u32[]{:S(2)}, u32[]{:S(2)}) collective-permute-start(bf16[2,48,1536]{2,1,0:T(8,128)(2,1)S(1)} %collective-permute-done.17), channel_id=1, source_target_pairs={{0,1},{1,2},{2,3},{3,4},{4,5},{5,6},{6,7},{7,8},{8,9},{9,10},{10,1... | collective-permute-start | bytes 884744 | tf_op jit(solution)/shard_map/ppermute | solution.py:79
  354.1 8.9 %collective-permute-start.25 = (bf16[2,48,1536]{2,1,0:T(8,128)(2,1)S(1)}, bf16[2,48,1536]{2,1,0:T(8,128)(2,1)S(1)}, u32[]{:S(2)}, u32[]{:S(2)}) collective-permute-start(bf16[2,48,1536]{2,1,0:T(8,128)(2,1)S(1)} %collective-permute-done.24), channel_id=1, source_target_pairs={{0,15},{1,0},{2,1},{3,2},{4,3},{5,4},{6,5},{7,6},{8,7},{9,8},{10,9... | collective-permute-start | bytes 884744 | tf_op jit(solution)/shard_map/ppermute | solution.py:81
  363.0 8.9 %collective-permute-start.19 = (bf16[2,48,1536]{2,1,0:T(8,128)(2,1)S(1)}, bf16[2,48,1536]{2,1,0:T(8,128)(2,1)S(1)}, u32[]{:S(2)}, u32[]{:S(2)}) collective-permute-start(bf16[2,48,1536]{2,1,0:T(8,128)(2,1)S(1)} %collective-permute-done.18), channel_id=1, source_target_pairs={{0,1},{1,2},{2,3},{3,4},{4,5},{5,6},{6,7},{7,8},{8,9},{9,10},{10,1... | collective-permute-start | bytes 884744 | tf_op jit(solution)/shard_map/ppermute | solution.py:79
  363.1 8.9 %collective-permute-start.26 = (bf16[2,48,1536]{2,1,0:T(8,128)(2,1)S(1)}, bf16[2,48,1536]{2,1,0:T(8,128)(2,1)S(1)}, u32[]{:S(2)}, u32[]{:S(2)}) collective-permute-start(bf16[2,48,1536]{2,1,0:T(8,128)(2,1)S(1)} %collective-permute-done.25), channel_id=1, source_target_pairs={{0,15},{1,0},{2,1},{3,2},{4,3},{5,4},{6,5},{7,6},{8,7},{9,8},{10,9... | collective-permute-start | bytes 884744 | tf_op jit(solution)/shard_map/ppermute | solution.py:81
  372.0 8.9 %collective-permute-start.20 = (bf16[2,48,1536]{2,1,0:T(8,128)(2,1)S(1)}, bf16[2,48,1536]{2,1,0:T(8,128)(2,1)S(1)}, u32[]{:S(2)}, u32[]{:S(2)}) collective-permute-start(bf16[2,48,1536]{2,1,0:T(8,128)(2,1)S(1)} %collective-permute-done.19), channel_id=1, source_target_pairs={{0,1},{1,2},{2,3},{3,4},{4,5},{5,6},{6,7},{7,8},{8,9},{9,10},{10,1... | collective-permute-start | bytes 884744 | tf_op jit(solution)/shard_map/ppermute | solution.py:79
  372.0 8.9 %collective-permute-start.27 = (bf16[2,48,1536]{2,1,0:T(8,128)(2,1)S(1)}, bf16[2,48,1536]{2,1,0:T(8,128)(2,1)S(1)}, u32[]{:S(2)}, u32[]{:S(2)}) collective-permute-start(bf16[2,48,1536]{2,1,0:T(8,128)(2,1)S(1)} %collective-permute-done.26), channel_id=1, source_target_pairs={{0,15},{1,0},{2,1},{3,2},{4,3},{5,4},{6,5},{7,6},{8,7},{9,8},{10,9... | collective-permute-start | bytes 884744 | tf_op jit(solution)/shard_map/ppermute | solution.py:81
  380.9 8.9 %collective-permute-start.21 = (bf16[2,48,1536]{2,1,0:T(8,128)(2,1)S(1)}, bf16[2,48,1536]{2,1,0:T(8,128)(2,1)S(1)}, u32[]{:S(2)}, u32[]{:S(2)}) collective-permute-start(bf16[2,48,1536]{2,1,0:T(8,128)(2,1)S(1)} %collective-permute-done.20), channel_id=1, source_target_pairs={{0,1},{1,2},{2,3},{3,4},{4,5},{5,6},{6,7},{7,8},{8,9},{9,10},{10,1... | collective-permute-start | bytes 884744 | tf_op jit(solution)/shard_map/ppermute | solution.py:79
  381.0 8.9 %collective-permute-start.28 = (bf16[2,48,1536]{2,1,0:T(8,128)(2,1)S(1)}, bf16[2,48,1536]{2,1,0:T(8,128)(2,1)S(1)}, u32[]{:S(2)}, u32[]{:S(2)}) collective-permute-start(bf16[2,48,1536]{2,1,0:T(8,128)(2,1)S(1)} %collective-permute-done.27), channel_id=1, source_target_pairs={{0,15},{1,0},{2,1},{3,2},{4,3},{5,4},{6,5},{7,6},{8,7},{9,8},{10,9... | collective-permute-start | bytes 884744 | tf_op jit(solution)/shard_map/ppermute | solution.py:81
  389.9 8.8 %collective-permute-start.22 = (bf16[2,48,1536]{2,1,0:T(8,128)(2,1)S(1)}, bf16[2,48,1536]{2,1,0:T(8,128)(2,1)S(1)}, u32[]{:S(2)}, u32[]{:S(2)}) collective-permute-start(bf16[2,48,1536]{2,1,0:T(8,128)(2,1)S(1)} %collective-permute-done.21), channel_id=1, source_target_pairs={{0,1},{1,2},{2,3},{3,4},{4,5},{5,6},{6,7},{7,8},{8,9},{9,10},{10,1... | collective-permute-start | bytes 884744 | tf_op jit(solution)/shard_map/ppermute | solution.py:79
  389.9 9.3 %collective-permute-start.29 = (bf16[2,48,1536]{2,1,0:T(8,128)(2,1)S(1)}, bf16[2,48,1536]{2,1,0:T(8,128)(2,1)S(1)}, u32[]{:S(2)}, u32[]{:S(2)}) collective-permute-start(bf16[2,48,1536]{2,1,0:T(8,128)(2,1)S(1)} %collective-permute-done.28), channel_id=1, source_target_pairs={{0,15},{1,0},{2,1},{3,2},{4,3},{5,4},{6,5},{7,6},{8,7},{9,8},{10,9... | collective-permute-start | bytes 884744 | tf_op jit(solution)/shard_map/ppermute | solution.py:81
  463.1 3.8 copy-start.2
Sparse Core Ops, SparseCore 0:
  20.3 78.2 reduce-scatter.6
  102.9 74.6 reduce-scatter.8
  409.1 53.9 all-gather.1
